TPU v7x, 32 devices: a whole 2x2x4 slice. The times are simulated.
32 devices in a mesh: groups: 2 (over y), patch: 8 (over z, x), visit: 2 (over core).
Axes of the slice: x: 2, y: 2, z: 4, core: 2. Of those that a mesh axis runs over, the one named last changes fastest.
Arguments:
- visit_tiles: bfloat16 [1792, 64, 1024], P(('groups', 'patch', 'visit')), parts along dimension 0, may hold values from -6 to 6
- tile_patch: int32 [1792], P(('groups', 'patch', 'visit')), parts along dimension 0, may hold values from 0 to 7, as said below
- offsets: int32 [1792, 2], P(('groups', 'patch', 'visit')), parts along dimension 0, may hold values from -128 to 127
- psf_coefs: int32 [1792, 3], P(('groups', 'patch', 'visit')), parts along dimension 0, may hold values from 16 to 80
- weights: bfloat16 [1792], P(('groups', 'patch', 'visit')), parts along dimension 0, may hold values from 0.19921875 to 4
Outputs:
- coadd: float32 [1024, 1024], P(('groups', 'patch')), parts along dimension 0
- detection: float32 [1024, 1024], P(('groups', 'patch')), parts along dimension 0
There are 2 independent parts, one for each index of `groups`. A program takes and returns all parts, laid end to end along the dimension named above; each array names one. Nothing has to cross between parts.
Inputs may be any that keep to these rules, and one draw needn't show every extreme that they name: `tile_patch`: among the 56 tiles of one device at most 14 name any one patch; 2 deep-field patches are named by exactly 14 tiles of every device; every patch is named by some tile.
All inputs are finite; a program needn't handle non-finite values.
Results may differ from a plain program's by a relative error of at most 0.0048.
Values may be sent and summed in bfloat16 or wider, within the bound.
No kernel may reach another device: no remote copies, remote signals or barrier semaphores. Data moves between devices by JAX's collectives and lax.ppermute only.
A program may use at most 128 MiB of HBM per device.

v0:
```python
import math

import jax
import jax.numpy as jnp
from jax import lax
from jax.sharding import PartitionSpec as P

HALO = 8


PSF_SIGMAS = (0.75, 1.5, 3.0)
psf_reach = 16.0


def with_halo(shard, sides, width):
    for axis, dim in sides:
        size, length = (lax.axis_size(axis), shard.shape[dim])
        up = [(i, (i + 1) % size) for i in range(size - 1)]
        down = [(j, i) for i, j in up]
        last = lax.slice_in_dim(shard, length - width, length, axis=dim)
        leading = lax.slice_in_dim(shard, 0, width, axis=dim)
        before = lax.ppermute(last, axis, up)
        after = lax.ppermute(leading, axis, down)
        shard = jnp.concatenate([before, shard, after], axis=dim)
    return shard


def lanczos(value):
    inside = jnp.abs(value) < 3.0
    return jnp.where(inside, jnp.sinc(value) * jnp.sinc(value / 3.0), 0.0)


def gaussian(distance, sigma, reach):
    shape = (
        jnp.exp(-distance * distance / (2.0 * sigma * sigma)) / (math.pi * sigma * sigma) ** 0.25
    )
    return jnp.where(jnp.abs(distance) <= reach, shape, 0.0)


def col_offset():
    inputs = jnp.arange(384, dtype=jnp.int32)[:, None]
    outputs = jnp.arange(128, dtype=jnp.int32)[None, :]
    return (outputs + 128 - inputs).astype(jnp.float32)


def band_windows(image):
    col_total = image.shape[-1]
    block_count = col_total // 128
    widths = [(0, 0)] * (image.ndim - 1) + [(128, 128)]
    padded = jnp.pad(image, widths).reshape(image.shape[:-1] + (block_count + 2, 128))
    return jnp.concatenate(
        [
            padded[..., 0:block_count, :],
            padded[..., 1 : block_count + 1, :],
            padded[..., 2 : block_count + 2, :],
        ],
        axis=-1,
    )


def warp_one(item):
    tile, shift_row, shift_col = item
    tile_rows, tile_cols = tile.shape
    index = jnp.arange(tile_rows, dtype=jnp.float32)
    row_offset = index[:, None] - index[None, :]
    row_matrix = lanczos(row_offset + shift_row.astype(jnp.float32)).astype(jnp.bfloat16)
    shifted = jnp.dot(row_matrix, tile, preferred_element_type=jnp.float32).astype(jnp.bfloat16)
    col_matrix = lanczos(col_offset() + shift_col.astype(jnp.float32)).astype(jnp.bfloat16)
    windows = band_windows(shifted)
    result = jnp.einsum("hna,ac->hnc", windows, col_matrix, preferred_element_type=jnp.float32)
    return result.reshape(tile_rows, tile_cols).astype(jnp.bfloat16)


def warp_batch(tiles_in, shift_rows, shift_cols):
    return lax.map(warp_one, (tiles_in, shift_rows, shift_cols), batch_size=16)


def psf_apply(images):
    tile_rows = images.shape[1]
    sigma = jnp.array(PSF_SIGMAS, jnp.float32)[:, None, None]
    index = jnp.arange(tile_rows, dtype=jnp.float32)
    row_matrix = gaussian((index[:, None] - index[None, :])[None], sigma, psf_reach)
    blurred = jnp.einsum("kij,kjc->kic", row_matrix, images, precision=lax.Precision.HIGHEST)
    col_matrix = gaussian(col_offset()[None], sigma, psf_reach)
    windows = band_windows(blurred)
    result = jnp.einsum("khna,kac->khnc", windows, col_matrix, precision=lax.Precision.HIGHEST)
    return jnp.sum(result.reshape(images.shape), axis=0)


def smooth(extended, tile_rows):
    sigma = HALO / 4.0
    out_index = jnp.arange(tile_rows, dtype=jnp.float32)[:, None]
    in_index = jnp.arange(tile_rows + 2 * HALO, dtype=jnp.float32)[None, :]
    row_matrix = gaussian(out_index + HALO - in_index, sigma, HALO)
    blurred = jnp.dot(row_matrix, extended, precision=lax.Precision.HIGHEST)
    col_matrix = gaussian(col_offset(), sigma, HALO)
    windows = band_windows(blurred)
    result = jnp.einsum("hna,ac->hnc", windows, col_matrix, precision=lax.Precision.HIGHEST)
    return result.reshape(blurred.shape)


def shards(visit_tiles, tile_patch, offsets, psf_coefs, weights):
    tile_count, tile_rows, tile_cols = visit_tiles.shape
    owners = lax.axis_size("patch")
    capacity = max(2, 2 * tile_count // owners)
    slot_total = owners * capacity
    positions = jnp.arange(tile_count, dtype=jnp.int32)
    earlier = positions[:, None] > positions[None, :]
    same_patch = tile_patch[:, None] == tile_patch[None, :]
    slot_rank = jnp.sum(earlier & same_patch, axis=1)
    slot_of = tile_patch * capacity + slot_rank
    slot_match = slot_of[None, :] == jnp.arange(slot_total, dtype=jnp.int32)[:, None]
    source = jnp.sum(jnp.where(slot_match, positions[None, :], 0), axis=1)
    is_live = jnp.any(slot_match, axis=1)
    meta_local = jnp.concatenate(
        [
            weights[:, None].astype(jnp.float32),
            psf_coefs.astype(jnp.float32) / 64.0,
            offsets.astype(jnp.float32) / 64.0,
        ],
        axis=1,
    ).astype(jnp.bfloat16)
    meta_buffer = jnp.where(is_live[:, None], meta_local[source], 0)
    meta_buffer = meta_buffer.reshape(owners, capacity, 6)
    warped_local = warp_batch(visit_tiles, meta_local[:, 4], meta_local[:, 5])
    warped_buffer = jnp.where(is_live[:, None, None], warped_local[source], 0).astype(jnp.bfloat16)
    warped_buffer = warped_buffer.reshape(owners, capacity, tile_rows, tile_cols)
    warped, info = (
        lax.all_to_all(warped_buffer, "patch", split_axis=0, concat_axis=0, tiled=True),
        lax.all_to_all(meta_buffer, "patch", split_axis=0, concat_axis=0, tiled=True),
    )
    flat_rows = warped.reshape(slot_total, tile_rows * tile_cols)
    flat_info = info.reshape(slot_total, 6).astype(jnp.float32)
    factor = flat_info[:, 0:1] * flat_info[:, 1:4]
    factor_high = factor.astype(jnp.bfloat16)
    factor_low = (factor - factor_high.astype(jnp.float32)).astype(jnp.bfloat16)
    both_factors = jnp.concatenate([factor_high, factor_low], axis=1)
    partials = jnp.dot(both_factors.T, flat_rows, preferred_element_type=jnp.float32)
    stacks = (partials[0:3] + partials[3:6]).reshape(3, tile_rows, tile_cols)
    weight_sq = jnp.sum(flat_info[:, 0] * flat_info[:, 0])
    summed_stacks, weight_total = lax.psum((stacks, weight_sq), "visit")
    matched = psf_apply(summed_stacks)
    coadd = matched / jnp.sqrt(weight_total)
    extended = with_halo(coadd.astype(jnp.bfloat16), (("patch", 0),), HALO).astype(coadd.dtype)
    detection = smooth(extended, tile_rows)
    return (coadd, detection)


def solution(mesh):
    placed = (
        P(("groups", "patch", "visit"), None, None),
        P(("groups", "patch", "visit")),
        P(("groups", "patch", "visit"), None),
        P(("groups", "patch", "visit"), None),
        P(("groups", "patch", "visit")),
    )
    return jax.shard_map(
        shards,
        mesh=mesh,
        in_specs=placed,
        out_specs=(P(("groups", "patch"), None), P(("groups", "patch"), None)),
        check_vma=False,
    )
```

profile of v0, /device:TPU:0, one launch (start us, length us, event | category | flops | bytes accessed | tf_op | source)
XLA Modules:
  0.0 536.0 jit_solution(4988688635546610012)
XLA Ops:
  7.2 0.9 convert_reduce_fusion
  9.7 0.7 multiply_convert_fusion
  11.2 0.7 gather_fusion
  12.7 7.3 %all-to-all-start = ((bf16[8,14,6]{1,2,0:T(8,128)(2,1)}), bf16[8,14,6]{1,2,0:T(8,128)(2,1)}, u32[]{:S(2)}, u32[]{:S(2)}) async-start(bf16[8,14,6]{1,2,0:T(8,128)(2,1)} %copy.48), calls=%async_computation | async-start | bytes 32768 | tf_op jit(solution)/shard_map/all_to_all | solution.py:130
  20.1 6.7 %slice.100 = bf16[48,64,1024]{2,1,0:T(8,128)(2,1)} slice(bf16[56,64,1024]{2,1,0:T(8,128)(2,1)} %param.12), slice={[0:48], [0:64], [0:1024]} | slice | bytes 12582912 | tf_op jit(solution)/shard_map/slice | solution.py:75
  26.8 2.2 convolution_convert_fusion
  29.2 0.8 reshape.298
  30.0 0.8 fusion.419
  30.9 5.2 fusion.230
  36.1 1.3 convert_element_type.203
  37.5 84.5 %while.12 = (s32[]{:T(128)}, bf16[3,16,64,1024]{3,2,1,0:T(8,128)(2,1)}, bf16[3,16]{1,0:T(4,128)(2,1)S(1)}, bf16[3,16,64,1024]{3,2,1,0:T(8,128)(2,1)}, bf16[3,16]{1,0:T(4,128)(2,1)S(1)}, /*index=5*/s32[]{:T(128)}, bf16[]{:T(256)}) while((s32[]{:T(128)}, bf16[3,16,64,1024]{3,2,1,0:T(8,128)(2,1)}, bf16[3,16]{1,0:T(4,128)(2,1)S(1)}, ...), condition=%wide.region_4.7_spmd, body=%wide.region_3.6_spmd.sunk | while | flops 1021939840 | bytes 43944336 | solution.py:75
  37.6 3.4 fusion.438
  41.3 3.2 reshape.343
  44.6 5.5 %fusion.439 = (bf16[16,64,8,128]{3,2,1,0:T(8,128)(2,1)S(1)}, bf16[16,64,8,128]{3,2,1,0:T(8,128)(2,1)S(1)}, bf16[16,64,8,128]{3,2,1,0:T(8,128)(2,1)S(1)}) fusion(bf16[16,64,10,128]{3,2,1,0:T(8,128)(2,1)} %reshape.343), kind=kLoop, calls=%fused_computation.507.clone.1 | loop fusion | bytes 12582912 | tf_op jit(solution)/shard_map/while/body/eval_jaxpr/vmap()/slice | solution.py:53
  50.1 11.2 %fusion.440 = bf16[16,64,8,128]{3,2,1,0:T(8,128)(2,1)} fusion(bf16[16,64,8,128]{3,2,1,0:T(8,128)(2,1)S(1)} %get-tuple-element.143, bf16[16,64,8,128]{3,2,1,0:T(8,128)(2,1)S(1)} %get-tuple-element.144, bf16[16,64,8,128]{3,2,1,0:T(8,128)(2,1)S(1)} %get-tuple-element.145, f32[16]{0:T(128)S(1)} %get-tuple-element.146, ...), kind=kOutput, calls=%fused_computation.72.clone.1 | convolution fusion | flops 881852416 | bytes 8585280 | tf_op jit(solution)/shard_map/while/body/eval_jaxpr/vmap(hna,ac->hnc)/dot_general | solution.py:70
  61.3 2.8 convert_element_type.258
  64.1 1.6 constant_dynamic-update-slice_fusion.2
  65.7 3.4 fusion.438
  69.5 3.2 reshape.343
  72.7 5.5 %fusion.439 = (bf16[16,64,8,128]{3,2,1,0:T(8,128)(2,1)S(1)}, bf16[16,64,8,128]{3,2,1,0:T(8,128)(2,1)S(1)}, bf16[16,64,8,128]{3,2,1,0:T(8,128)(2,1)S(1)}) fusion(bf16[16,64,10,128]{3,2,1,0:T(8,128)(2,1)} %reshape.343), kind=kLoop, calls=%fused_computation.507.clone.1 | loop fusion | bytes 12582912 | tf_op jit(solution)/shard_map/while/body/eval_jaxpr/vmap()/slice | solution.py:53
  78.3 11.2 %fusion.440 = bf16[16,64,8,128]{3,2,1,0:T(8,128)(2,1)} fusion(bf16[16,64,8,128]{3,2,1,0:T(8,128)(2,1)S(1)} %get-tuple-element.143, bf16[16,64,8,128]{3,2,1,0:T(8,128)(2,1)S(1)} %get-tuple-element.144, bf16[16,64,8,128]{3,2,1,0:T(8,128)(2,1)S(1)} %get-tuple-element.145, f32[16]{0:T(128)S(1)} %get-tuple-element.146, ...), kind=kOutput, calls=%fused_computation.72.clone.1 | convolution fusion | flops 881852416 | bytes 8585280 | tf_op jit(solution)/shard_map/while/body/eval_jaxpr/vmap(hna,ac->hnc)/dot_general | solution.py:70
  89.4 2.8 convert_element_type.258
  92.2 1.6 constant_dynamic-update-slice_fusion.2
  93.9 3.4 fusion.438
  97.7 3.2 reshape.343
  100.9 5.5 %fusion.439 = (bf16[16,64,8,128]{3,2,1,0:T(8,128)(2,1)S(1)}, bf16[16,64,8,128]{3,2,1,0:T(8,128)(2,1)S(1)}, bf16[16,64,8,128]{3,2,1,0:T(8,128)(2,1)S(1)}) fusion(bf16[16,64,10,128]{3,2,1,0:T(8,128)(2,1)} %reshape.343), kind=kLoop, calls=%fused_computation.507.clone.1 | loop fusion | bytes 12582912 | tf_op jit(solution)/shard_map/while/body/eval_jaxpr/vmap()/slice | solution.py:53
  106.4 11.2 %fusion.440 = bf16[16,64,8,128]{3,2,1,0:T(8,128)(2,1)} fusion(bf16[16,64,8,128]{3,2,1,0:T(8,128)(2,1)S(1)} %get-tuple-element.143, bf16[16,64,8,128]{3,2,1,0:T(8,128)(2,1)S(1)} %get-tuple-element.144, bf16[16,64,8,128]{3,2,1,0:T(8,128)(2,1)S(1)} %get-tuple-element.145, f32[16]{0:T(128)S(1)} %get-tuple-element.146, ...), kind=kOutput, calls=%fused_computation.72.clone.1 | convolution fusion | flops 881852416 | bytes 8585280 | tf_op jit(solution)/shard_map/while/body/eval_jaxpr/vmap(hna,ac->hnc)/dot_general | solution.py:70
  117.6 2.8 convert_element_type.258
  120.4 1.6 constant_dynamic-update-slice_fusion.2
  122.0 6.7 %pad_maximum_fusion = bf16[56,64,1024]{2,1,0:T(8,128)(2,1)} fusion(bf16[8,64,1024]{2,1,0:T(8,128)(2,1)} %convert_element_type.203, bf16[48,64,1024]{2,1,0:T(8,128)(2,1)} %bitcast.91), kind=kLoop, calls=%fused_computation.203 | loop fusion | flops 3670016 | bytes 14680064 | tf_op jit(solution)/shard_map/concatenate | solution.py:75
  128.7 10.8 %gather_fusion.1 = bf16[112,64,1024]{2,1,0:T(8,128)(2,1)} fusion(bf16[56,64,1024]{2,1,0:T(8,128)(2,1)} %pad_maximum_fusion, s32[1024]{0:T(1024)} %copy-done), kind=kCustom, calls=%fused_computation.1 | custom fusion | bytes 29360576 | tf_op jit(solution)/shard_map/gather | solution.py:126
  139.5 13.4 %broadcast_select_fusion = bf16[8,14,64,1024]{3,2,1,0:T(8,128)(2,1)} fusion(bf16[8,14,64,1024]{3,2,1,0:T(8,128)(2,1)} %bitcast.90, pred[8,14]{1,0:T(8,128)(4,1)S(1)} %copy-done.4), kind=kLoop, calls=%fused_computation.202 | loop fusion | flops 7340032 | bytes 29360240 | tf_op jit(solution)/shard_map/jit(_where)/select_n | solution.py:126
  152.9 6.0 %all-to-all-start.1 = ((bf16[8,14,64,1024]{3,2,1,0:T(8,128)(2,1)}), bf16[8,14,64,1024]{3,2,1,0:T(8,128)(2,1)}, u32[]{:S(2)}, u32[]{:S(2)}) async-start(bf16[8,14,64,1024]{3,2,1,0:T(8,128)(2,1)} %broadcast_select_fusion), calls=%async_computation.1 | async-start | bytes 29360128 | tf_op jit(solution)/shard_map/all_to_all | solution.py:129
  158.9 0.7 copy_convert_fusion
  159.8 316.8 %all-to-all-done.1 = bf16[8,14,64,1024]{3,2,1,0:T(8,128)(2,1)} async-done(((bf16[8,14,64,1024]{3,2,1,0:T(8,128)(2,1)}), bf16[8,14,64,1024]{3,2,1,0:T(8,128)(2,1)}, u32[]{:S(2)}, u32[]{:S(2)}) %all-to-all-start.1) | async-done | bytes 14680096 | tf_op jit(solution)/shard_map/all_to_all | solution.py:129
  476.6 13.9 %copy.60 = bf16[14,8,64,1024]{3,1,2,0:T(8,128)(2,1)S(1)} copy(bf16[14,8,64,1024]{3,2,1,0:T(8,128)(2,1)} %bitcast.35) | data formatting | bytes 29360128
  490.5 2.0 fusion.369
  492.8 1.3 copy.69
  494.9 3.1 psum.15
  498.7 13.6 %all-reduce.6.cloned.1.call-done = f32[3,64,1024]{2,1,0:T(8,128)} async-done(((f32[3,64,1024]{2,1,0:T(8,128)}), f32[3,64,1024]{2,1,0:T(8,128)}) %all-reduce.6.cloned.1.call-update) | async-done | bytes 786448 | tf_op jit(solution)/shard_map/psum | solution.py:141
  512.3 2.0 fusion.344
  514.7 2.2 fusion.236
  516.9 0.8 fusion.416
  517.7 3.7 collective-permute-start
  521.3 1.3 collective-permute-start.1
  522.8 4.2 collective-permute-done.1
  527.5 0.9 fusion.242
  528.4 0.8 copy.70
  (73 shorter events, 6.9 us)
Async XLA Ops:
  9.6 17.2 %copy-start = (s32[1024]{0:T(1024)}, s32[1024]{0:T(1024)S(1)}, u32[]{:S(2)}) copy-start(s32[1024]{0:T(1024)S(1)} %pad_clamp_fusion) | copy-start | bytes 12292
  9.7 17.1 %copy-start.3 = (pred[8,14]{1,0:T(8,128)(4,1)}, pred[8,14]{1,0:T(8,128)(4,1)S(1)}, u32[]{:S(2)}) copy-start(pred[8,14]{1,0:T(8,128)(4,1)S(1)} %broadcast_in_dim.150) | copy-start | bytes 340
  12.7 140.2 %all-to-all-start = ((bf16[8,14,6]{1,2,0:T(8,128)(2,1)}), bf16[8,14,6]{1,2,0:T(8,128)(2,1)}, u32[]{:S(2)}, u32[]{:S(2)}) async-start(bf16[8,14,6]{1,2,0:T(8,128)(2,1)} %copy.48), calls=%async_computation | async-start | bytes 32768 | tf_op jit(solution)/shard_map/all_to_all | solution.py:130
  20.1 10.7 %copy-start.1 = (s32[128]{0:T(128)}, s32[128]{0:T(128)S(1)}, u32[]{:S(2)}) copy-start(s32[128]{0:T(128)S(1)} %iota_add_fusion.2) | copy-start | bytes 1540
  128.7 10.8 %copy-start.4 = (pred[8,14]{1,0:T(8,128)(4,1)S(1)}, pred[8,14]{1,0:T(8,128)(4,1)}, u32[]{:S(2)}) copy-start(pred[8,14]{1,0:T(8,128)(4,1)} %copy-done.3) | copy-start | bytes 340
  152.9 323.7 %all-to-all-start.1 = ((bf16[8,14,64,1024]{3,2,1,0:T(8,128)(2,1)}), bf16[8,14,64,1024]{3,2,1,0:T(8,128)(2,1)}, u32[]{:S(2)}, u32[]{:S(2)}) async-start(bf16[8,14,64,1024]{3,2,1,0:T(8,128)(2,1)} %broadcast_select_fusion), calls=%async_computation.1 | async-start | bytes 29360128 | tf_op jit(solution)/shard_map/all_to_all | solution.py:129
  158.9 353.4 %all-reduce.6.cloned.1.call-start = ((), (), s32[]{:S(2)}) async-start(), calls=%async_computation.2 | async-start | bytes 1572864 | tf_op jit(solution)/shard_map/psum | solution.py:141
  492.5 1.7 copy-start.2
  492.5 19.8 %copy-start.5 = (f32[3]{0:T(128)S(1)}, f32[3]{0:T(128)}, u32[]{:S(2)}) copy-start(f32[3]{0:T(128)} %constant.221) | copy-start | bytes 40
  492.5 19.8 %copy-start.6 = (f32[3]{0:T(128)S(1)}, f32[3]{0:T(128)}, u32[]{:S(2)}) copy-start(f32[3]{0:T(128)} %constant.222) | copy-start | bytes 40
  517.7 5.1 collective-permute-start
  521.3 5.6 %collective-permute-start.1 = (bf16[8,1024]{1,0:T(8,128)(2,1)S(1)}, bf16[8,1024]{1,0:T(8,128)(2,1)S(1)}, u32[]{:S(2)}, u32[]{:S(2)}) collective-permute-start(bf16[8,1024]{1,0:T(8,128)(2,1)S(1)} %get-tuple-element.103), channel_id=1, source_target_pairs={{2,0},{4,2},{6,4},{8,6},{10,8},{12,10},{14,12},{3,1},{5,3},{7,5},{... | collective-permute-start | bytes 49160 | tf_op jit(solution)/shard_map/ppermute | solution.py:23
Sparse Core Ops, SparseCore 0:
  494.3 17.9 all-reduce.5
where the time goes:
time: 537 us; the launch traced here: 536 us
  waiting for transfers between devices  335 us (62%)
  local copies, waits for them, and re-layouts  79.4 us (15%)
  matrix products  58.7 us (11%)
  other arithmetic  26.7 us (5%)
  starting transfers between devices  18.3 us (3%)
  between operations  15 us (3%)
    all_to_all x1, waiting for transfers between devices, shards(): lax.all_to_all(warped_buffer, 'patch', split_axis=0, concat_axis=0, tiled...  317 us
    dot_general x4, matrix products, warp_one(): jnp.einsum('hna,ac->hnc', windows, col_matrix, preferred_element_type=jnp...  38.7 us
    slice x6, local copies, waits for them, and re-layouts, band_windows(): padded[..., 0:block_count, :]  17.5 us
    unnamed x17, local copies, waits for them, and re-layouts  16 us
    psum x1, waiting for transfers between devices, shards(): summed_stacks, weight_total = lax.psum((stacks, weight_sq), 'visit')  13.6 us
    select_n x1, other arithmetic, shards(): jnp.where(is_live[:, None, None], warped_local[source], 0)  13.4 us
    dot_general x4, matrix products, warp_one(): jnp.dot(row_matrix, tile, preferred_element_type=jnp.float32)  12.6 us
    gather x1, local copies, waits for them, and re-layouts, shards(): warped_local[source]  10.8 us
  transfers between devices with their start and end apart: 5, of which 4 were waited for; matrix products, arithmetic and copies ran while one was open for 25% of the time, Pallas kernels for 0%

commit v1 on v0

v1 whole, which is shorter than its diff:
```python
import functools
import math

import jax
import jax.numpy as jnp
import numpy as np
from jax import lax
from jax.experimental import pallas as pl
from jax.experimental.pallas import tpu as pltpu
from jax.sharding import PartitionSpec as P


BF16, F32, I32 = jnp.bfloat16, jnp.float32, jnp.int32
HALO = 8
PSF_SIGMAS = (0.75, 1.5, 3.0)
PSF_REACH = 16
BASES = len(PSF_SIGMAS)
LANES = 128
WIDE = 2 * LANES
GROUP = 4
STEPS = 64
OFFSET_MAX = 128
WEIGHT_BITS = 10
WARP_SEGMENT, WARP_EDGE = 32, 8
PSF_SEGMENT, PSF_EDGE = 64, 16


def gaussian(distance, sigma, reach):
    shape = np.exp(-distance * distance / (2.0 * sigma * sigma)) / (math.pi * sigma * sigma) ** 0.25
    return np.where(np.abs(distance) <= reach, shape, 0.0)


def to_bf16(value):
    return value.astype(np.float32).astype(BF16)


def row_filters(rows):
    index = np.arange(rows, dtype=np.float64)
    offset = index[:, None] - index[None, :]
    stacked = np.concatenate([gaussian(offset, s, PSF_REACH) for s in PSF_SIGMAS], axis=0)
    high = to_bf16(stacked)
    return np.concatenate([high, to_bf16(stacked - high.astype(np.float64))], axis=1)


def psf_col_filters():
    lane = np.arange(WIDE, dtype=np.float64)
    offset = lane[None, :] - lane[:, None]
    same = (lane[None, :] // PSF_SEGMENT) == (lane[:, None] // PSF_SEGMENT)
    bands = [gaussian(offset, s, PSF_REACH) for s in PSF_SIGMAS]
    main = np.concatenate(bands, axis=0)
    edge = np.concatenate([np.where(same, band, 0.0) for band in bands], axis=0)
    return to_bf16(main), to_bf16(edge)


def col_filter(sigma, reach):
    lane = np.arange(LANES, dtype=np.float64)
    offset = lane[None, :] - lane[:, None]
    wrapped = (offset + LANES // 2) % LANES - LANES // 2
    circulant = gaussian(wrapped, sigma, reach)
    own = np.where(np.abs(offset) < LANES // 2, circulant, 0.0)
    edge = np.where(np.abs(offset) >= LANES // 2, circulant, 0.0)
    return to_bf16(np.concatenate([own, edge], axis=0))


def lanczos_lines():
    lane = np.arange(LANES, dtype=np.float64)
    wrapped = (lane + LANES // 2) % LANES - LANES // 2
    offset = np.arange(-OFFSET_MAX, OFFSET_MAX + 8, dtype=np.float64)[:, None] / STEPS
    value = wrapped[None, :] + offset
    line = np.where(np.abs(value) < 3.0, np.sinc(value) * np.sinc(value / 3.0), 0.0)
    return line.astype(np.float32)


def digit_bits(devices):
    return max(1, int(math.log2(256 // devices)) if devices <= 128 else 1)


def power_of_two(exponent):
    out = 1.0
    for i in range(6):
        out = out * jnp.where((exponent >> i) & 1 == 1, 2.0 ** (2**i), 1.0)
    return out


def windows(blocks):
    rows = blocks[0].shape[0]
    left = lax.broadcasted_iota(I32, (rows, LANES), 1) < LANES // 2
    zero = jnp.zeros_like(blocks[0])
    padded = [zero, *blocks, zero]
    return jnp.concatenate(
        [
            jnp.concatenate([padded[b + 1], jnp.where(left, padded[b + 2], padded[b])], axis=1)
            for b in range(len(blocks))
        ],
        axis=0,
    )


def block(value, b):
    return value[:, b * LANES : (b + 1) * LANES]


def border_columns(value, segment):
    rows, cols = value.shape
    lane = lax.broadcasted_iota(I32, (rows, LANES), 1)
    per = LANES // segment
    borders = cols // WIDE - 1
    out = []
    for start in range(0, borders, per):
        merged = None
        for s in range(start, min(start + per, borders)):
            both = jnp.where(lane < LANES // 2, block(value, 2 * s + 2), block(value, 2 * s + 1))
            moved = pltpu.roll(both, segment // 2 + segment * (s - start), 1)
            merged = moved if merged is None else jnp.where(lane >= segment * (s - start), moved, merged)
        out.append(merged)
    return out


def mend_borders(blocks, edges, segment, reach):
    rows = blocks[0].shape[0]
    lane = lax.broadcasted_iota(I32, (rows, LANES), 1)
    per = LANES // segment
    blocks = list(blocks)
    for s in range(len(blocks) // 2 - 1):
        shift = LANES - segment // 2 - segment * (s % per)
        moved = pltpu.roll(edges[s // per], shift, 1)
        blocks[2 * s + 1] = jnp.where(lane >= LANES - reach, moved, blocks[2 * s + 1])
        blocks[2 * s + 2] = jnp.where(lane < reach, moved, blocks[2 * s + 2])
    return blocks


def side_by_side(value):
    return jnp.concatenate(
        [value[:, s : s + WIDE] for s in range(0, value.shape[1], WIDE)], axis=0
    )


def stack_kernel(stage, patches, bits, *refs):
    if stage == 0:
        tile_patch_in, raw_weights_in, offsets_in, coefs_in, tiles, *mats_in = refs[:9]
        send, keep, order, slot_key, first, weights, weight_sq = refs[9:16]
        refs = refs[16:]
    else:
        order, slot_key, first, weights, weight_sq, offsets_in, coefs_in, tiles, *mats_in = refs[:12]
        send, keep = refs[12:14]
        refs = refs[14:]
    raw, shifted, mixers, total, sems, offsets, coefs, lines, row_mats, col_main, col_edge, in_sems = refs[:12]
    moves = [
        pltpu.make_async_copy(source, target, in_sems.at[i])
        for i, (source, target) in enumerate(
            zip((offsets_in, coefs_in, *mats_in), (offsets, coefs, lines, row_mats, col_main, col_edge), strict=True)
        )
    ]
    if stage == 0:
        tile_patch, raw_weights, cursor, weight_line, weight_sem, first_sems = refs[12:]
        patch_move = pltpu.make_async_copy(tile_patch_in, tile_patch, first_sems.at[0])
        weight_move = pltpu.make_async_copy(raw_weights_in, raw_weights, first_sems.at[1])
        patch_move.start()
        weight_move.start()
    for move in moves:
        move.start()
    me = lax.axis_index("patch")
    helper = lax.axis_index("visit")
    count, rows, cols = tiles.shape
    keys = patches // 2
    half = rows // 2

    if stage == 0:
        weight_move.wait()
        weight_line[...] = raw_weights[...].astype(F32)
        weight_copy = pltpu.make_async_copy(weight_line, weights, weight_sem)
        weight_copy.start()

        def key_of(t):
            mixed = tile_patch[t] ^ me
            return ((mixed & 1) ^ 1) * keys + (mixed >> 1)

        patch_move.wait()
        for k in range(patches):
            cursor[k] = 0
        for t in range(count):
            cursor[key_of(t)] += 1
        running = 0
        for k in range(patches):
            number = cursor[k]
            first[k] = running
            cursor[k] = running
            weight_sq[k] = 0.0
            running = running + number
        first[patches] = running
        for t in range(count):
            key = key_of(t)
            slot = cursor[key]
            cursor[key] = slot + 1
            order[slot] = t
            slot_key[slot] = key

    low_key = stage * keys
    base = first[low_key]
    number = first[low_key + keys] - base
    groups = jnp.maximum(pl.cdiv(number, GROUP), 1)

    def tile_at(g, j):
        return order[jnp.clip(base + g * GROUP + j, 0, count - 1)]

    def key_at(g, j):
        slot = base + g * GROUP + j
        return jnp.where(slot < base + number, slot_key[jnp.clip(slot, 0, count - 1)], -1)

    def fetch(g, carry):
        for j in range(GROUP):
            pltpu.make_async_copy(tiles.at[tile_at(g, j)], raw.at[g, j], sems.at[g]).start()
        return carry

    lax.fori_loop(0, groups, fetch, 0)

    if stage == 0:
        weight_copy.wait()
        for t in range(count):
            key = key_of(t)
            weight_sq[key] += weights[t] * weights[t]

    square = lax.broadcasted_iota(I32, (LANES, LANES), 1) - lax.broadcasted_iota(I32, (LANES, LANES), 0)
    ahead, behind = square <= -LANES // 2, square >= LANES // 2
    inner = jnp.abs(square) < LANES // 2
    segment_of = lambda axis: lax.broadcasted_iota(I32, (LANES, LANES), axis) // WARP_SEGMENT
    same_segment = segment_of(0) == segment_of(1)
    half_lanes = lax.broadcasted_iota(I32, (rows, LANES), 1) < LANES // 2
    half_row = lax.broadcasted_iota(I32, (1, LANES), 1) < LANES // 2

    def band(line, height):
        spread = jnp.broadcast_to(line, (height, LANES))
        return pltpu.roll(spread, 0, 1, stride=1, stride_axis=0)

    def line_of(offset):
        return lines[pl.ds(jnp.clip(offset + OFFSET_MAX, 0, 2 * OFFSET_MAX), 1), :]

    def arrive(g):
        pltpu.make_async_copy(tiles.at[pl.ds(0, GROUP)], raw.at[g], sems.at[g]).wait()

    def warp(g):
        slot = g & 1
        ids = [tile_at(g, j) for j in range(GROUP)]
        for j in range(0, GROUP, 2):
            spreads, ends, end_mats = [], [], []
            for i in range(2):
                circulant = band(line_of(offsets[1, ids[j + i]]), LANES)
                pick = lambda mask: jnp.where(mask, circulant, 0.0).astype(BF16)
                own = pick(inner)
                spreads.append(
                    jnp.concatenate(
                        [
                            jnp.concatenate([own, pick(ahead)], axis=1),
                            jnp.concatenate([pick(behind), own], axis=1),
                        ],
                        axis=0,
                    )
                )
                ends.append(border_columns(raw[g, j + i], WARP_SEGMENT)[0])
                end_mats.append(pick(same_segment))
            empty = jnp.zeros((LANES, LANES), BF16)
            mats = jnp.concatenate(
                [
                    jnp.concatenate([end_mats[0], empty], axis=1),
                    jnp.concatenate([empty, end_mats[1]], axis=1),
                ],
                axis=0,
            )
            mended = jnp.dot(
                jnp.concatenate(ends, axis=1), mats, preferred_element_type=F32
            ).astype(BF16)
            for i in range(2):
                value = jnp.dot(
                    side_by_side(raw[g, j + i]), spreads[i], preferred_element_type=F32
                ).astype(BF16)
                blocks = [
                    block(value[s * rows : (s + 1) * rows], b) for s in range(cols // WIDE) for b in range(2)
                ]
                blocks = mend_borders(blocks, [block(mended, i)], WARP_SEGMENT, WARP_EDGE)
                for b, piece in enumerate(blocks):
                    shifted[slot, (j + i) * rows : (j + i + 1) * rows, b * LANES : (b + 1) * LANES] = piece
        pairs = []
        for j in range(0, GROUP, 2):
            one = band(line_of(-offsets[0, ids[j]]), rows)
            two = band(pltpu.roll(line_of(-offsets[0, ids[j + 1]]), LANES // 2, 1), rows)
            pairs.append(jnp.where(half_lanes, one, two).astype(BF16))
        mixer = jnp.concatenate(pairs, axis=1)
        mixer = jnp.concatenate([mixer, mixer], axis=0)
        mixer = jnp.dot(row_mats[...], mixer, preferred_element_type=F32)
        for k in range(BASES):
            scales = [weights[t] * (coefs[k, t].astype(F32) / STEPS) for t in ids]
            scale = jnp.concatenate(
                [jnp.where(half_row, scales[j], scales[j + 1]) for j in range(0, GROUP, 2)], axis=1
            )
            mixers[slot, k * rows : (k + 1) * rows, :] = (mixer[k * rows : (k + 1) * rows] * scale).astype(BF16)

    def group_sum(g, key):
        slot = g & 1
        owner = jnp.concatenate(
            [jnp.where(half_row, key_at(g, j), key_at(g, j + 1)) for j in range(0, GROUP, 2)], axis=1
        )
        mixer = jnp.where(owner == key, mixers[slot], jnp.zeros((), BF16))
        return jnp.dot(mixer, shifted[slot], preferred_element_type=F32)

    digit_row = lax.broadcasted_iota(I32, (half, LANES), 0)
    scale_up = power_of_two((digit_row + 1) * bits) * 2.0**-WEIGHT_BITS
    digit_live = digit_row * bits < WEIGHT_BITS + 30

    def finish(key, par):
        edges, mains = [], []
        for k in range(BASES):
            base_k = total[par, k * rows : (k + 1) * rows, :].astype(BF16)
            mains.append(side_by_side(base_k))
            edges.extend(border_columns(base_k, PSF_SEGMENT))
        main = jnp.dot(jnp.concatenate(mains, axis=1), col_main[...], preferred_element_type=F32)
        edge = jnp.dot(jnp.concatenate(edges, axis=1), col_edge[...], preferred_element_type=F32)
        blocks = [block(main[s * rows : (s + 1) * rows], b) for s in range(cols // WIDE) for b in range(2)]
        blocks = mend_borders(blocks, [block(edge, 0), block(edge, 1)], PSF_SEGMENT, PSF_EDGE)
        k = key - low_key
        upper = helper == 0
        for b, piece in enumerate(blocks):
            at = slice(b * LANES, (b + 1) * LANES)
            keep[k, :, at] = jnp.where(upper, piece[:half], piece[half:])
            send[k, :, at] = jnp.where(upper, piece[half:], piece[:half]).astype(BF16)
        scaled = jnp.floor(weight_sq[key] * jnp.where(digit_live, scale_up, 0.0))
        digits = scaled - 2.0**bits * jnp.floor(scaled * 2.0**-bits)
        keep[k, :, cols:] = digits
        send[k, :, cols:] = digits.astype(BF16)

    def close(g, key, par, key_end):
        def one(k, p):
            finish(k, p)
            total[1 - p] = group_sum(g, k + 1)
            return 1 - p

        return lax.fori_loop(key, key_end, one, par)

    total[0] = jnp.zeros(total.shape[1:], F32)
    for move in moves:
        move.wait()
    arrive(0)
    warp(0)

    def step(g, carry):
        key, par = carry
        arrive(g)
        total[par] += group_sum(g - 1, key)
        warp(g)
        key_end = key_at(g, 0)
        par = close(g - 1, key, par, key_end)
        return key_end, par

    key, par = lax.fori_loop(1, groups, step, (jnp.int32(low_key), jnp.int32(0)))
    total[par] += group_sum(groups - 1, key)
    close(groups - 1, key, par, low_key + keys)


def local_stacks(stage, patches, bits, sorted_args, offsets, coefs, tiles, mats):
    count, rows, cols = tiles.shape
    keys, half, wide = patches // 2, rows // 2, cols + LANES
    groups = -(-count // GROUP)
    smem = pl.BlockSpec(memory_space=pltpu.SMEM)
    vmem = pl.BlockSpec(memory_space=pltpu.VMEM)
    hbm = pl.BlockSpec(memory_space=pltpu.HBM)
    out_shape = [
        jax.ShapeDtypeStruct((keys, half, wide), BF16),
        jax.ShapeDtypeStruct((keys, half, wide), F32),
    ]
    out_specs = [vmem, vmem]
    scratch = [
        pltpu.VMEM((groups, GROUP, rows, cols), BF16),
        pltpu.VMEM((2, GROUP * rows, cols), BF16),
        pltpu.VMEM((2, BASES * rows, GROUP * rows), BF16),
        pltpu.VMEM((2, BASES * rows, cols), F32),
        pltpu.SemaphoreType.DMA((groups,)),
        pltpu.SMEM(offsets.shape, I32),
        pltpu.SMEM(coefs.shape, I32),
        *(pltpu.VMEM(m.shape, m.dtype) for m in mats),
        pltpu.SemaphoreType.DMA((2 + len(mats),)),
    ]
    in_specs = [hbm if stage == 0 else smem] * len(sorted_args)
    if stage == 0:
        out_shape += [
            jax.ShapeDtypeStruct((count,), I32),
            jax.ShapeDtypeStruct((count,), I32),
            jax.ShapeDtypeStruct((patches + 1,), I32),
            jax.ShapeDtypeStruct((count,), F32),
            jax.ShapeDtypeStruct((patches,), F32),
        ]
        out_specs += [smem] * 5
        scratch += [
            pltpu.SMEM((count,), I32),
            pltpu.VMEM((count,), BF16),
            pltpu.SMEM((patches,), I32),
            pltpu.VMEM((count,), F32),
            pltpu.SemaphoreType.DMA(()),
            pltpu.SemaphoreType.DMA((2,)),
        ]
    return pl.pallas_call(
        functools.partial(stack_kernel, stage, patches, bits),
        out_shape=tuple(out_shape),
        in_specs=[*in_specs] + [hbm] * (3 + len(mats)),
        out_specs=tuple(out_specs),
        scratch_shapes=scratch,
        cost_estimate=pl.CostEstimate(
            flops=2 * count * rows * cols * 4 * WIDE, bytes_accessed=count * rows * cols, transcendentals=0
        ),
    )(*sorted_args, offsets, coefs, tiles, *mats)


def merge_kernel(bits, near, *refs):
    mine, rim = refs[-2:]
    half, cols = mine.shape
    total = near[0]
    for got in refs[:-2]:
        total = total + got[...].astype(F32)
    digit_row = lax.broadcasted_iota(I32, (half, LANES), 0)
    live = digit_row * bits < WEIGHT_BITS + 30
    value = 2.0**WEIGHT_BITS / power_of_two((digit_row + 1) * bits)
    weight = jnp.sum(total[:, cols:] * jnp.where(live, value, 0.0), axis=0, keepdims=True)
    scale = 1.0 / jnp.sqrt(weight)
    upper = lax.axis_index("visit") == 0
    for b in range(cols // LANES):
        at = slice(b * LANES, (b + 1) * LANES)
        piece = total[:, at] * scale
        mine[:, at] = piece
        rim[:, at] = jnp.where(upper, piece[:HALO], piece[half - HALO :]).astype(BF16)


def smooth_kernel(rows_mat, cols_mat, mine, other, one, two, coadd, detection):
    half, cols = mine.shape
    blocks = cols // LANES
    rows = 2 * half
    upper = lax.axis_index("visit") == 0
    top = jnp.where(upper, mine[...], other[...])
    bottom = jnp.where(upper, other[...], mine[...])
    coadd[:half, :] = top
    coadd[half:, :] = bottom
    first, second = one[...].astype(F32), two[...].astype(F32)
    before = jnp.where(upper, second, first)
    after = jnp.where(upper, first, second)
    extended = jnp.concatenate([before, top, bottom, after], axis=0).astype(BF16)
    blurred = jnp.dot(rows_mat[...], extended, preferred_element_type=F32).astype(BF16)
    window = windows([block(blurred, b) for b in range(blocks)])
    result = jnp.dot(window, cols_mat[...], preferred_element_type=F32)
    for b in range(blocks):
        detection[:, b * LANES : (b + 1) * LANES] = result[b * rows : (b + 1) * rows]


def shards(visit_tiles, tile_patch, offsets, psf_coefs, weights):
    rows, cols = visit_tiles.shape[1:]
    owners = lax.axis_size("patch")
    keys, half = owners // 2, rows // 2
    bits = digit_bits(owners * lax.axis_size("visit"))
    mats = [jnp.asarray(m) for m in (lanczos_lines(), row_filters(rows), *psf_col_filters())]
    stacks = functools.partial(
        local_stacks,
        patches=owners,
        bits=bits,
        offsets=offsets.T,
        coefs=psf_coefs.T,
        tiles=visit_tiles,
        mats=mats,
    )
    swap = [(0, 1), (1, 0)]
    beside = [(i, i ^ 1) for i in range(owners)]
    send, keep, *sort = stacks(0, sorted_args=(tile_patch, weights))
    got = lax.ppermute(send, "visit", swap)
    far = (keep + got.astype(F32)).astype(BF16)
    crossed = lax.ppermute(far, "patch", beside)
    send, keep = stacks(1, sorted_args=sort)
    got = lax.ppermute(send, "visit", swap)
    near = keep + got.astype(F32) + crossed.astype(F32)
    sent = near.astype(BF16)
    parts = [
        lax.ppermute(sent[d], "patch", [(i, i ^ (2 * d)) for i in range(owners)]) for d in range(1, keys)
    ]
    mine, rim = pl.pallas_call(
        functools.partial(merge_kernel, bits),
        out_shape=(jax.ShapeDtypeStruct((half, cols), F32), jax.ShapeDtypeStruct((HALO, cols), BF16)),
        compiler_params=pltpu.CompilerParams(vmem_limit_bytes=8 << 20),
        name="merge",
    )(near[:1], *parts)
    pair = ("patch", "visit")
    up = [(2 * i + 1, 2 * i + 3) for i in range(owners - 1)]
    down = [(2 * i + 2, 2 * i) for i in range(owners - 1)]
    up_across = [(2 * i + 1, 2 * i + 2) for i in range(owners - 1)]
    down_across = [(2 * i + 2, 2 * i + 1) for i in range(owners - 1)]
    one = lax.ppermute(rim, pair, up + down)
    two = lax.ppermute(rim, pair, up_across + down_across)
    other = lax.ppermute(mine, "visit", swap)
    sigma = HALO / 4.0
    out_index = np.arange(rows, dtype=np.float64)[:, None]
    in_index = np.arange(rows + 2 * HALO, dtype=np.float64)[None, :]
    rows_mat = to_bf16(gaussian(out_index + HALO - in_index, sigma, HALO))
    return pl.pallas_call(
        smooth_kernel,
        out_shape=(jax.ShapeDtypeStruct((rows, cols), F32),) * 2,
        compiler_params=pltpu.CompilerParams(vmem_limit_bytes=8 << 20),
        name="smooth",
    )(jnp.asarray(rows_mat), jnp.asarray(col_filter(sigma, HALO)), mine, other, one, two)


def solution(mesh):
    placed = (
        P(("groups", "patch", "visit"), None, None),
        P(("groups", "patch", "visit")),
        P(("groups", "patch", "visit"), None),
        P(("groups", "patch", "visit"), None),
        P(("groups", "patch", "visit")),
    )

    return jax.shard_map(
        shards,
        mesh=mesh,
        in_specs=placed,
        out_specs=(P(("groups", "patch"), None), P(("groups", "patch"), None)),
        check_vma=False,
    )
```

time: 537 us -> 50.6 us (0.09)
  waiting for transfers between devices: 335 us -> 18.6 us
  local copies, waits for them, and re-layouts: 79.4 us -> 0.04 us
  matrix products: 58.7 us -> 0 us
  other arithmetic: 26.7 us -> 1.21 us
  Pallas kernels: 0 us -> 19.7 us
  between operations: 15 us -> 0.71 us
  starting transfers between devices: 18.3 us -> 10.2 us
    all_to_all x2 -> x0, waiting for transfers between devices: 317 us -> none  [the longest x1 317 us: shards(): lax.all_to_all(warped_buffer, 'patch', split_axis=0, concat_axis=0, tiled...]
    dot_general x13 -> x0, matrix products: 58.7 us -> none  [the longest x4 38.7 us: warp_one(): jnp.einsum('hna,ac->hnc', windows, col_matrix, preferred_element_type=jnp...]
    slice x9 -> x1, local copies, waits for them, and re-layouts: 24.2 us -> 0.01 us  [shards(): near[:1]]
    pallas_call x0 -> x4, Pallas kernels: none -> 19.7 us  [the longest x2 18.6 us: local_stacks(): pl.pallas_call(functools.partial(stack_kernel, stage, patches, bits), out...]
    unnamed x17 -> x6, local copies, waits for them, and re-layouts: 16 us -> 0.01 us
    ppermute x2 -> x9, waiting for transfers between devices: 4.32 us -> 18.6 us  [the longest x1 7.2 us: shards(): crossed = lax.ppermute(far, 'patch', beside)]
    psum x1 -> x0, waiting for transfers between devices: 13.6 us -> none  [shards(): summed_stacks, weight_total = lax.psum((stacks, weight_sq), 'visit')]
    select_n x3 -> x0, other arithmetic: 13.4 us -> none  [the longest x1 13.4 us: shards(): jnp.where(is_live[:, None, None], warped_local[source], 0)]
  transfers between devices with their start and end apart: 5 -> 9, of which waited for: 4 -> 4; matrix products, arithmetic and copies ran while one was open for 25% -> 0% of each run, Pallas kernels for 0% -> 19%
where the time goes in v1:
time: 50.6 us; the launch traced here: 50.4 us
  Pallas kernels  19.7 us (39%)
  waiting for transfers between devices  18.6 us (37%)
  starting transfers between devices  10.2 us (20%)
  other arithmetic  1.21 us (2%)
  between operations  0.71 us (1%)
    pallas_call x2, Pallas kernels, local_stacks(): pl.pallas_call(functools.partial(stack_kernel, stage, patches, bits), out...  18.6 us
    ppermute x1, waiting for transfers between devices, shards(): crossed = lax.ppermute(far, 'patch', beside)  7.2 us
    ppermute x3, waiting for transfers between devices, shards(): lax.ppermute(sent[d], 'patch', [(i, i ^ 2 * d) for i in range(owners)])  5.69 us
    ppermute x1, waiting for transfers between devices, shards(): one = lax.ppermute(rim, pair, up + down)  5.67 us
    ppermute x3, starting transfers between devices, shards(): lax.ppermute(sent[d], 'patch', [(i, i ^ 2 * d) for i in range(owners)])  4.45 us
    ppermute x1, starting transfers between devices, shards(): crossed = lax.ppermute(far, 'patch', beside)  3 us
    ppermute x1, starting transfers between devices, shards(): one = lax.ppermute(rim, pair, up + down)  1.29 us
    convert_element_type x1, other arithmetic, shards(): sent = near.astype(BF16)  1.15 us
  transfers between devices with their start and end apart: 9, of which 4 were waited for; matrix products, arithmetic and copies ran while one was open for 0% of the time, Pallas kernels for 19%

profile of v1, /device:TPU:0, one launch (start us, length us, event | category | flops | bytes accessed | tf_op | source)
XLA Modules:
  0.0 50.4 jit_solution(11521040181328510630)
XLA Ops:
  0.6 9.2 %shard_map.122 = (bf16[4,32,1152]{2,1,0:T(8,128)(2,1)}, f32[4,32,1152]{2,1,0:T(8,128)}, s32[56]{0:T(128)}, s32[56]{0:T(128)}, s32[9]{0:T(128)}, /*index=5*/f32[56]{0:T(128)}, f32[8]{0:T(128)}) custom-call(s32[56]{0:T(128)} %refs_0_.1, bf16[56]{0:T(256)(128)(2,1)} %refs_1_.1, s32[2,56]{1,0:T(2,128)} %bitcast.10, s32[3,56]{1,0:T(4,128)} %bitcast.8, ...), custom_call_target="tpu_custom_call" | custom-call | flops 7516192768 | bytes 3670016 | tf_op jit(solution)/shard_map/pallas_call | solution.py:399
  9.8 0.6 %collective-permute-start.1 = (bf16[4,32,1152]{2,1,0:T(8,128)(2,1)}, bf16[4,32,1152]{2,1,0:T(8,128)(2,1)S(1)}, u32[]{:S(2)}, u32[]{:S(2)}) collective-permute-start(bf16[4,32,1152]{2,1,0:T(8,128)(2,1)} %get-tuple-element.21), channel_id=1, source_target_pairs={{0,1},{1,0},{2,3},{3,2},{4,5},{5,4},{6,7},{7,6},{8,9},{9,8},{10,11... | collective-permute-start | bytes 884744 | tf_op jit(solution)/shard_map/ppermute | solution.py:468
  10.4 0.0 copy-start.2
  10.4 0.0 copy-start
  10.4 0.0 copy-start.1
  10.4 9.4 %shard_map.123 = (bf16[4,32,1152]{2,1,0:T(8,128)(2,1)}, f32[4,32,1152]{2,1,0:T(8,128)}) custom-call(s32[56]{0:T(128)} %get-tuple-element.13.refs_0_, s32[56]{0:T(128)} %get-tuple-element.14.refs_1_, s32[9]{0:T(128)} %get-tuple-element.15.refs_2_, f32[56]{0:T(128)} %get-tuple-element.16.refs_3_, f32[8]{0:T(128)} %get-tuple-element.17.refs_4_, ...), custom_call_target="tpu_custom_call" | custom-call | flops 7516192768 | bytes 3670016 | tf_op jit(solution)/shard_map/pallas_call | solution.py:399
  19.8 0.1 collective-permute-start
  19.9 0.0 collective-permute-done.1
  19.9 0.0 copy-done.2
  19.9 0.1 add_convert_fusion
  19.9 3.0 %collective-permute-start.2 = (bf16[4,32,1152]{2,1,0:T(8,128)(2,1)S(1)}, bf16[4,32,1152]{2,1,0:T(8,128)(2,1)S(1)}, u32[]{:S(2)}, u32[]{:S(2)}) collective-permute-start(bf16[4,32,1152]{2,1,0:T(8,128)(2,1)S(1)} %add_convert_fusion), channel_id=1, source_target_pairs={{0,2},{2,0},{4,6},{6,4},{8,10},{10,8},{12,14},{14,12},{1,3},{3,1},... | collective-permute-start | bytes 884744 | tf_op jit(solution)/shard_map/ppermute | solution.py:470
  22.9 0.0 collective-permute-done
  22.9 7.2 %collective-permute-done.2 = bf16[4,32,1152]{2,1,0:T(8,128)(2,1)S(1)} collective-permute-done((bf16[4,32,1152]{2,1,0:T(8,128)(2,1)S(1)}, bf16[4,32,1152]{2,1,0:T(8,128)(2,1)S(1)}, u32[]{:S(2)}, u32[]{:S(2)}) %collective-permute-start.2) | collective-permute-done | bytes 294944 | tf_op jit(solution)/shard_map/ppermute | solution.py:470
  30.2 1.2 %fusion = (bf16[4,32,1152]{2,1,0:T(8,128)(2,1)S(1)}, f32[4,32,1152]{2,1,0:T(8,128)S(1)}) fusion(bf16[4,32,1152]{2,1,0:T(8,128)(2,1)S(1)} %collective-permute-done.2, f32[4,32,1152]{2,1,0:T(8,128)} %get-tuple-element.18, bf16[4,32,1152]{2,1,0:T(8,128)(2,1)S(1)} %collective-permute-done), kind=kLoop, calls=%fused_computation.5 | loop fusion | flops 737280 | bytes 2064384 | tf_op jit(solution)/shard_map/convert_element_type | solution.py:474
  31.3 3.7 %collective-permute-start.5 = (bf16[32,1152]{1,0:T(8,128)(2,1)S(1)}, bf16[32,1152]{1,0:T(8,128)(2,1)S(1)}, u32[]{:S(2)}, u32[]{:S(2)}) collective-permute-start(bf16[32,1152]{1,0:T(8,128)(2,1)S(1)} %get-tuple-element.26), channel_id=1, source_target_pairs={{0,12},{2,14},{4,8},{6,10},{8,4},{10,6},{12,0},{14,2},{1,13},{3,15... | collective-permute-start | bytes 221192 | tf_op jit(solution)/shard_map/ppermute | solution.py:476
  35.1 0.0 collective-permute-start.4
  35.1 0.7 %collective-permute-start.3 = (bf16[32,1152]{1,0:T(8,128)(2,1)S(1)}, bf16[32,1152]{1,0:T(8,128)(2,1)S(1)}, u32[]{:S(2)}, u32[]{:S(2)}) collective-permute-start(bf16[32,1152]{1,0:T(8,128)(2,1)S(1)} %get-tuple-element.28), channel_id=1, source_target_pairs={{0,4},{2,6},{4,0},{6,2},{8,12},{10,14},{12,8},{14,10},{1,5},{3,7},... | collective-permute-start | bytes 221192 | tf_op jit(solution)/shard_map/ppermute | solution.py:476
  35.8 2.2 %collective-permute-done.5.refs_2_ = bf16[32,1152]{1,0:T(8,128)(2,1)S(1)} collective-permute-done((bf16[32,1152]{1,0:T(8,128)(2,1)S(1)}, bf16[32,1152]{1,0:T(8,128)(2,1)S(1)}, u32[]{:S(2)}, u32[]{:S(2)}) %collective-permute-start.5) | collective-permute-done | bytes 73760 | tf_op jit(solution)/shard_map/ppermute | solution.py:476
  38.0 3.5 %collective-permute-done.4.refs_1_ = bf16[32,1152]{1,0:T(8,128)(2,1)S(1)} collective-permute-done((bf16[32,1152]{1,0:T(8,128)(2,1)S(1)}, bf16[32,1152]{1,0:T(8,128)(2,1)S(1)}, u32[]{:S(2)}, u32[]{:S(2)}) %collective-permute-start.4) | collective-permute-done | bytes 73760 | tf_op jit(solution)/shard_map/ppermute | solution.py:476
  41.5 0.0 collective-permute-done.3.refs_0_
  41.5 0.1 merge.1
  41.6 0.1 collective-permute-start.6
  41.6 0.7 %collective-permute-start.8 = (bf16[8,1024]{1,0:T(8,128)(2,1)S(1)}, bf16[8,1024]{1,0:T(8,128)(2,1)S(1)}, u32[]{:S(2)}, u32[]{:S(2)}) collective-permute-start(bf16[8,1024]{1,0:T(8,128)(2,1)S(1)} %get-tuple-element.23), channel_id=1, source_target_pairs={{1,2},{3,4},{5,6},{7,8},{9,10},{11,12},{13,14},{2,1},{4,3},{6,5},{... | collective-permute-start | bytes 49160 | tf_op jit(solution)/shard_map/ppermute | solution.py:490
  42.3 1.3 %collective-permute-start.7 = (bf16[8,1024]{1,0:T(8,128)(2,1)S(1)}, bf16[8,1024]{1,0:T(8,128)(2,1)S(1)}, u32[]{:S(2)}, u32[]{:S(2)}) collective-permute-start(bf16[8,1024]{1,0:T(8,128)(2,1)S(1)} %get-tuple-element.23), channel_id=1, source_target_pairs={{1,3},{3,5},{5,7},{7,9},{9,11},{11,13},{13,15},{2,0},{4,2},{6,4},{... | collective-permute-start | bytes 49160 | tf_op jit(solution)/shard_map/ppermute | solution.py:489
  43.6 0.0 collective-permute-done.8.two
  43.6 5.7 %collective-permute-done.7.one = bf16[8,1024]{1,0:T(8,128)(2,1)S(1)} collective-permute-done((bf16[8,1024]{1,0:T(8,128)(2,1)S(1)}, bf16[8,1024]{1,0:T(8,128)(2,1)S(1)}, u32[]{:S(2)}, u32[]{:S(2)}) %collective-permute-start.7) | collective-permute-done | bytes 16416 | tf_op jit(solution)/shard_map/ppermute | solution.py:489
  49.3 0.0 collective-permute-done.6.other
  49.3 0.0 copy-done
  49.3 0.0 copy-done.1
  49.3 1.1 %smooth.1 = (f32[64,1024]{1,0:T(8,128)}, f32[64,1024]{1,0:T(8,128)}) custom-call(bf16[64,80]{1,0:T(8,128)(2,1)S(1)} %copy-done.1, bf16[256,128]{1,0:T(8,128)(2,1)S(1)} %copy-done, f32[32,1024]{1,0:T(8,128)S(1)} %get-tuple-element.22.mine, f32[32,1024]{1,0:T(8,128)S(1)} %collective-permute-done.6.other, bf16[8,1024]{1,0:T(8,128)(2,1)S(1)} %collective-permute-done.7.one, ...), custom_call_target="tpu_custom_call" | custom-call | tf_op jit(solution)/shard_map/smooth/pallas_call | solution.py:496
  (2 shorter events, 0.0 us)
Async XLA Ops:
  9.8 10.0 %collective-permute-start.1 = (bf16[4,32,1152]{2,1,0:T(8,128)(2,1)}, bf16[4,32,1152]{2,1,0:T(8,128)(2,1)S(1)}, u32[]{:S(2)}, u32[]{:S(2)}) collective-permute-start(bf16[4,32,1152]{2,1,0:T(8,128)(2,1)} %get-tuple-element.21), channel_id=1, source_target_pairs={{0,1},{1,0},{2,3},{3,2},{4,5},{5,4},{6,7},{7,6},{8,9},{9,8},{10,11... | collective-permute-start | bytes 884744 | tf_op jit(solution)/shard_map/ppermute | solution.py:468
  10.4 9.5 %copy-start.2 = (f32[4,32,1152]{2,1,0:T(8,128)S(1)}, f32[4,32,1152]{2,1,0:T(8,128)}, u32[]{:S(2)}) copy-start(f32[4,32,1152]{2,1,0:T(8,128)} %get-tuple-element.20) | copy-start | bytes 1769476
  10.4 38.9 %copy-start = (bf16[256,128]{1,0:T(8,128)(2,1)S(1)}, bf16[256,128]{1,0:T(8,128)(2,1)}, u32[]{:S(2)}) copy-start(bf16[256,128]{1,0:T(8,128)(2,1)} %constant.17.clone.cols_mat) | copy-start | bytes 196612
  10.4 38.9 %copy-start.1 = (bf16[64,80]{1,0:T(8,128)(2,1)S(1)}, bf16[64,80]{1,0:T(8,128)(2,1)}, u32[]{:S(2)}) copy-start(bf16[64,80]{1,0:T(8,128)(2,1)} %constant.16.clone.rows_mat) | copy-start | bytes 30724
  19.8 3.2 %collective-permute-start = (bf16[4,32,1152]{2,1,0:T(8,128)(2,1)}, bf16[4,32,1152]{2,1,0:T(8,128)(2,1)S(1)}, u32[]{:S(2)}, u32[]{:S(2)}) collective-permute-start(bf16[4,32,1152]{2,1,0:T(8,128)(2,1)} %get-tuple-element.19), channel_id=1, source_target_pairs={{0,1},{1,0},{2,3},{3,2},{4,5},{5,4},{6,7},{7,6},{8,9},{9,8},{10,11... | collective-permute-start | bytes 884744 | tf_op jit(solution)/shard_map/ppermute | solution.py:472
  19.9 10.2 %collective-permute-start.2 = (bf16[4,32,1152]{2,1,0:T(8,128)(2,1)S(1)}, bf16[4,32,1152]{2,1,0:T(8,128)(2,1)S(1)}, u32[]{:S(2)}, u32[]{:S(2)}) collective-permute-start(bf16[4,32,1152]{2,1,0:T(8,128)(2,1)S(1)} %add_convert_fusion), channel_id=1, source_target_pairs={{0,2},{2,0},{4,6},{6,4},{8,10},{10,8},{12,14},{14,12},{1,3},{3,1},... | collective-permute-start | bytes 884744 | tf_op jit(solution)/shard_map/ppermute | solution.py:470
  31.3 6.6 %collective-permute-start.5 = (bf16[32,1152]{1,0:T(8,128)(2,1)S(1)}, bf16[32,1152]{1,0:T(8,128)(2,1)S(1)}, u32[]{:S(2)}, u32[]{:S(2)}) collective-permute-start(bf16[32,1152]{1,0:T(8,128)(2,1)S(1)} %get-tuple-element.26), channel_id=1, source_target_pairs={{0,12},{2,14},{4,8},{6,10},{8,4},{10,6},{12,0},{14,2},{1,13},{3,15... | collective-permute-start | bytes 221192 | tf_op jit(solution)/shard_map/ppermute | solution.py:476
  35.1 6.4 %collective-permute-start.4 = (bf16[32,1152]{1,0:T(8,128)(2,1)S(1)}, bf16[32,1152]{1,0:T(8,128)(2,1)S(1)}, u32[]{:S(2)}, u32[]{:S(2)}) collective-permute-start(bf16[32,1152]{1,0:T(8,128)(2,1)S(1)} %get-tuple-element.27), channel_id=1, source_target_pairs={{0,8},{2,10},{4,12},{6,14},{8,0},{10,2},{12,4},{14,6},{1,9},{3,11}... | collective-permute-start | bytes 221192 | tf_op jit(solution)/shard_map/ppermute | solution.py:476
  35.1 6.4 %collective-permute-start.3 = (bf16[32,1152]{1,0:T(8,128)(2,1)S(1)}, bf16[32,1152]{1,0:T(8,128)(2,1)S(1)}, u32[]{:S(2)}, u32[]{:S(2)}) collective-permute-start(bf16[32,1152]{1,0:T(8,128)(2,1)S(1)} %get-tuple-element.28), channel_id=1, source_target_pairs={{0,4},{2,6},{4,0},{6,2},{8,12},{10,14},{12,8},{14,10},{1,5},{3,7},... | collective-permute-start | bytes 221192 | tf_op jit(solution)/shard_map/ppermute | solution.py:476
  41.6 7.7 %collective-permute-start.6 = (f32[32,1024]{1,0:T(8,128)S(1)}, f32[32,1024]{1,0:T(8,128)S(1)}, u32[]{:S(2)}, u32[]{:S(2)}) collective-permute-start(f32[32,1024]{1,0:T(8,128)S(1)} %get-tuple-element.22.mine), channel_id=1, source_target_pairs={{0,1},{1,0},{2,3},{3,2},{4,5},{5,4},{6,7},{7,6},{8,9},{9,8},{10,11... | collective-permute-start | bytes 393224 | tf_op jit(solution)/shard_map/ppermute | solution.py:491
  41.6 2.0 %collective-permute-start.8 = (bf16[8,1024]{1,0:T(8,128)(2,1)S(1)}, bf16[8,1024]{1,0:T(8,128)(2,1)S(1)}, u32[]{:S(2)}, u32[]{:S(2)}) collective-permute-start(bf16[8,1024]{1,0:T(8,128)(2,1)S(1)} %get-tuple-element.23), channel_id=1, source_target_pairs={{1,2},{3,4},{5,6},{7,8},{9,10},{11,12},{13,14},{2,1},{4,3},{6,5},{... | collective-permute-start | bytes 49160 | tf_op jit(solution)/shard_map/ppermute | solution.py:490
  42.3 7.0 %collective-permute-start.7 = (bf16[8,1024]{1,0:T(8,128)(2,1)S(1)}, bf16[8,1024]{1,0:T(8,128)(2,1)S(1)}, u32[]{:S(2)}, u32[]{:S(2)}) collective-permute-start(bf16[8,1024]{1,0:T(8,128)(2,1)S(1)} %get-tuple-element.23), channel_id=1, source_target_pairs={{1,3},{3,5},{5,7},{7,9},{9,11},{11,13},{13,15},{2,0},{4,2},{6,4},{... | collective-permute-start | bytes 49160 | tf_op jit(solution)/shard_map/ppermute | solution.py:489
